TPU v7x, 128 devices: a whole 4x4x4 slice. The times are simulated.
128 devices in a mesh: cascade: 2 (over y_lo), coil: 8 (over z, core), readout: 8 (over x, y_hi).
Axes of the slice: x: 4, y: 4 (y_hi: 2, y_lo: 2; y = y_hi * 2 + y_lo), z: 4, core: 2. Of those that a mesh axis runs over, the one named last changes fastest.
Arguments:
- initial: bfloat16 [2, 4, 16, 128, 2, 128], P(None, None, 'readout'), may hold values from -6 to 6
- coil_maps: bfloat16 [2, 16, 16, 128, 2, 128], P(None, 'coil', 'readout'), may hold values from -1.5 to 1.5
- kspace: bfloat16 [2, 16, 4, 16, 128, 2, 128], P(None, 'coil', None, 'readout'), may hold values from -6 to 6
- sampled: int32 [16, 4, 128, 128], P('coil'), may hold values 0 or 1
- first_w: bfloat16 [2, 27, 2, 64], P('cascade'), may hold values from -0.875 to 0.875
- time_w: bfloat16 [2, 3, 64, 64], P('cascade'), may hold values from -0.4375 to 0.4375
- last_w: bfloat16 [2, 27, 64, 2], P('cascade'), may hold values from -0.15625 to 0.15625
Outputs:
- images: bfloat16 [2, 2, 4, 16, 128, 2, 128], P('cascade', None, None, 'readout', 'coil')
Inputs may be any that keep to these rules, and one draw needn't show every extreme that they name: `sampled`: 1 where the sample at that phase, line and partition was acquired for that coil, else 0.
All inputs are finite; a program needn't handle non-finite values. No bound on the sum of `sampled` on one device may be relied on, other than what follows from the above.
Results may differ from a plain program's by a relative error of at most 0.024.
Values may be sent and summed in bfloat16 or wider, within the bound.
A program may use at most 128 MiB of HBM per device.

v0:
```python
import jax
import jax.numpy as jnp
from jax import lax
from jax.sharding import PartitionSpec as P


def extended(block, sides, width):
    for axis, dim in sides:
        count = lax.axis_size(axis)
        forward = [(i, i + 1) for i in range(count - 1)]
        backward = [(target, source) for source, target in forward]
        low = lax.ppermute(
            lax.slice_in_dim(block, block.shape[dim] - width, None, axis=dim), axis, forward
        )
        high = lax.ppermute(lax.slice_in_dim(block, 0, width, axis=dim), axis, backward)
        block = jnp.concatenate([low, block, high], axis=dim)
    return block


def shifted(block, axis, distance):
    devices = range(lax.axis_size(axis))
    route = [(i - distance, i) for i in devices if i - distance in devices]
    return lax.ppermute(block, axis, route)


def fourier_table(length, direction):
    positions = jnp.arange(length, dtype=jnp.int32)
    products = positions[:, None] * positions[None, :] % length
    angles = products.astype(jnp.float32) * (2.0 * jnp.pi / length)
    factor = 1.0 / jnp.sqrt(jnp.float32(length))
    return (jnp.cos(angles) * factor, direction * jnp.sin(angles) * factor)


def row_matrix(length, direction):
    cosine_part, sine_part = fourier_table(length, direction)
    blocks = jnp.stack(
        [jnp.stack([cosine_part, -sine_part], -1), jnp.stack([sine_part, cosine_part], -1)], 1
    )
    return blocks.reshape(2 * length, 2 * length).astype(jnp.bfloat16)


def column_matrix(length, direction):
    cosine_part, sine_part = fourier_table(length, direction)
    blocks = jnp.stack(
        [jnp.stack([cosine_part, sine_part], 1), jnp.stack([-sine_part, cosine_part], 1)], 0
    )
    return blocks.reshape(2 * length, 2 * length).astype(jnp.bfloat16)


def multiply(coil_map, values, conjugate):
    coil_map = coil_map.astype(jnp.float32)
    values = values.astype(jnp.float32)
    map_real, map_imag = (coil_map[..., 0, :], coil_map[..., 1, :])
    value_real, value_imag = (values[..., 0, :], values[..., 1, :])
    if conjugate:
        return jnp.stack(
            [
                map_real * value_real + map_imag * value_imag,
                map_real * value_imag - map_imag * value_real,
            ],
            -2,
        )
    return jnp.stack(
        [
            map_real * value_real - map_imag * value_imag,
            map_real * value_imag + map_imag * value_real,
        ],
        -2,
    )


def along_columns(fields, matrix):
    layout = fields.shape
    flattened = fields.reshape(-1, 2 * layout[-1])
    return jnp.dot(flattened, matrix, preferred_element_type=jnp.float32).reshape(layout)


def along_rows(fields, matrix):
    layout = fields.shape
    flattened = fields.reshape(-1, 2 * layout[-3], layout[-1])
    result = jnp.einsum("ab,nbz->naz", matrix, flattened, preferred_element_type=jnp.float32)
    return result.reshape(layout)


def lift(padded, weights):
    row_count = padded.shape[1] - 2
    line_count = padded.shape[2] - 2
    part_count = padded.shape[4] - 2
    tap_views = [
        padded[
            :,
            row_shift : row_shift + row_count,
            line_shift : line_shift + line_count,
            :,
            part_shift : part_shift + part_count,
        ]
        for row_shift in range(3)
        for line_shift in range(3)
        for part_shift in range(3)
    ]
    stacked = jnp.stack(tap_views, 3)
    stacked = stacked.reshape(stacked.shape[0], row_count, line_count, -1, part_count)
    return jnp.einsum(
        "prlie,io->prloe",
        stacked,
        weights.reshape(-1, weights.shape[-1]),
        preferred_element_type=jnp.float32,
    )


def temporal(hidden, weights):
    phase_count = hidden.shape[0]
    padded = jnp.pad(hidden, ((2, 2), (0, 0), (0, 0), (0, 0), (0, 0)))
    total = hidden.astype(jnp.float32)
    for tap_index in range(3):
        total = total + jnp.einsum(
            "prlie,io->prloe",
            padded[2 * tap_index : 2 * tap_index + phase_count],
            weights[tap_index],
            preferred_element_type=jnp.float32,
        )
    return jax.nn.relu(total).astype(jnp.bfloat16)


def project(edged, weights, base):
    row_count = edged.shape[1] - 2
    line_count = edged.shape[2] - 2
    part_count = edged.shape[4]
    per_tap = jnp.einsum("prlie,tio->prltoe", edged, weights, preferred_element_type=jnp.float32)
    per_tap = jnp.pad(per_tap, ((0, 0), (0, 0), (0, 0), (0, 0), (0, 0), (1, 1)))
    total = base.astype(jnp.float32)
    for row_shift in range(3):
        for line_shift in range(3):
            for part_shift in range(3):
                tap_index = 9 * row_shift + 3 * line_shift + part_shift
                total = (
                    total
                    + per_tap[
                        :,
                        row_shift : row_shift + row_count,
                        line_shift : line_shift + line_count,
                        tap_index,
                        :,
                        part_shift : part_shift + part_count,
                    ]
                )
    return total.astype(jnp.bfloat16)


def cascade(image, coil_maps, measured, sampled, first_w, time_w, last_w, tables):
    forward_rows, forward_columns, inverse_rows, inverse_columns = tables
    coil_image = multiply(coil_maps[:, None], image[None], False).astype(jnp.bfloat16)
    half_done = along_columns(coil_image, forward_columns).astype(jnp.bfloat16)
    spectrum = along_rows(half_done, forward_rows)
    weight = sampled.astype(jnp.float32)[:, :, None, :, None, :]
    mixed = (spectrum + weight * (measured.astype(jnp.float32) - spectrum)).astype(jnp.bfloat16)
    back_half = along_rows(mixed, inverse_rows).astype(jnp.bfloat16)
    restored = along_columns(back_half, inverse_columns)
    terms = jnp.sum(multiply(coil_maps[:, None], restored, True), axis=0)
    summed = lax.psum(terms.astype(jnp.bfloat16), "coil").astype(jnp.float32)
    line_share = summed.shape[2] // lax.axis_size("coil")
    combined = lax.dynamic_slice_in_dim(summed, lax.axis_index("coil") * line_share, line_share, 2)
    combined = combined.astype(jnp.bfloat16)
    padded = extended(combined, (("coil", 2), ("readout", 1)), 1)
    padded = jnp.pad(padded, ((0, 0), (0, 0), (0, 0), (0, 0), (1, 1)))
    hidden = jax.nn.relu(lift(padded, first_w)).astype(jnp.bfloat16)
    mixed_time = temporal(hidden, time_w)
    edged = extended(mixed_time, (("coil", 2), ("readout", 1)), 1)
    return project(edged, last_w, combined)


def per_device(initial, coil_maps, kspace, sampled, first_w, time_w, last_w):
    section_no = lax.axis_index("cascade")
    micro_count = kspace.shape[0]
    line_total = kspace.shape[4]
    part_total = kspace.shape[6]
    tables = (
        row_matrix(line_total, -1.0),
        column_matrix(part_total, -1.0),
        row_matrix(line_total, 1.0),
        column_matrix(part_total, 1.0),
    )
    line_share = line_total // lax.axis_size("coil")
    single = initial[0]
    tick_count = micro_count + lax.axis_size("cascade") - 1
    results = jnp.zeros(
        (1, micro_count, single.shape[0], single.shape[1], line_share, 2, part_total), jnp.bfloat16
    )
    carried = jnp.zeros_like(single)
    for tick_index in range(tick_count):
        position = tick_index - section_no
        valid = (position >= 0) & (position < micro_count)
        picked = jnp.clip(position, 0, micro_count - 1)
        start_image = lax.dynamic_index_in_dim(initial, picked, 0, False)
        image = jnp.where(section_no == 0, start_image, carried)
        block_maps = lax.dynamic_index_in_dim(coil_maps, picked, 0, False)
        block_data = lax.dynamic_index_in_dim(kspace, picked, 0, False)
        output = cascade(
            image, block_maps, block_data, sampled, first_w[0], time_w[0], last_w[0], tables
        )
        updated = lax.dynamic_update_index_in_dim(results, output[None, None], picked, 1)
        results = jnp.where(valid, updated, results)
        if tick_index < tick_count - 1:
            assembled = lax.all_gather(output, "coil", axis=2, tiled=True)
            carried = shifted(assembled, "cascade", 1)
    return results


def solution(mesh):
    in_specs = (
        P(None, None, "readout", None, None, None),
        P(None, "coil", "readout", None, None, None),
        P(None, "coil", None, "readout", None, None, None),
        P("coil", None, None, None),
        P("cascade", None, None, None),
        P("cascade", None, None, None),
        P("cascade", None, None, None),
    )
    out_specs = P("cascade", None, None, "readout", "coil", None, None)
    return jax.shard_map(
        per_device, mesh=mesh, in_specs=in_specs, out_specs=out_specs, check_vma=False
    )
```

profile of v0, /device:TPU:35, one launch (start us, length us, event | category | flops | bytes accessed | tf_op | source)
XLA Modules:
  0.0 706.0 jit_solution(2028351478313013722)
XLA Ops:
  25.7 6.2 copy.131
  31.9 13.1 %reshape.464 = bf16[256,256,1]{1,0,2:T(8,128)(2,1)S(1)} reshape(bf16[128,2,128,2]{3,2,1,0:T(8,128)(2,1)} %copy.131) | data formatting | bytes 262144 | tf_op jit(solution)/shard_map/convert_element_type | solution.py:39
  45.0 6.2 copy.135
  51.2 13.8 %reshape.465 = bf16[256,256,1]{1,0,2:T(8,128)(2,1)} reshape(bf16[128,2,128,2]{3,2,1,0:T(8,128)(2,1)} %copy.135) | data formatting | bytes 262144 | tf_op jit(solution)/shard_map/convert_element_type | solution.py:39
  82.9 59.1 %all-reduce.13.cloned.1.call-done = bf16[4,2,128,2,128]{4,3,2,1,0:T(2,128)(2,1)} async-done(((bf16[4,2,128,2,128]{4,3,2,1,0:T(2,128)(2,1)}), bf16[4,2,128,2,128]{4,3,2,1,0:T(2,128)(2,1)}) %all-reduce.13.cloned.1.call-update) | async-done | bytes 524304 | tf_op jit(solution)/shard_map/psum | solution.py:160
  142.9 4.0 collective-permute-start
  152.1 4.6 collective-permute-start.2
  176.5 4.3 collective-permute-done.5
  183.3 3.9 collective-permute-start.6
  191.0 47.2 %collective-permute-done.6 = bf16[4,1,18,64,128]{4,3,2,1,0:T(8,128)(2,1)} collective-permute-done((bf16[4,1,18,64,128]{4,3,2,1,0:T(8,128)(2,1)}, bf16[4,1,18,64,128]{4,3,2,1,0:T(8,128)(2,1)}, u32[]{:S(2)}, u32[]{:S(2)}) %collective-permute-start.6) | collective-permute-done | bytes 1179680 | tf_op jit(solution)/shard_map/ppermute | solution.py:12
  245.0 9.6 %copy.146 = f32[4,4,18,27,2,128]{5,4,2,1,0,3:T(2,128)S(1)} copy(f32[4,4,18,27,2,128]{5,3,4,2,1,0:T(8,128)S(1)} %fusion.33) | data formatting | bytes 15925248 | tf_op jit(solution)/shard_map/prlie,tio->prltoe/transpose | solution.py:129
  258.3 13.3 %all_gather.6 = bf16[4,2,128,2,128]{4,3,2,1,0:T(2,128)(2,1)} all-gather(bf16[4,2,16,2,128]{4,3,2,1,0:T(2,128)(2,1)S(1)} %get-tuple-element.8), channel_id=1, replica_groups=mesh['cascade'=2,'coil'=8,'readout'=8] {'coil'}, dimensions={2}, use_global_device_ids=true | all-gather | bytes 589824 | tf_op jit(solution)/shard_map/all_gather | solution.py:204
  279.9 5.3 collective-permute-done.8
  302.9 60.0 %all-reduce.15.cloned.1.call-done = bf16[4,2,128,2,128]{4,3,2,1,0:T(2,128)(2,1)} async-done(((bf16[4,2,128,2,128]{4,3,2,1,0:T(2,128)(2,1)}), bf16[4,2,128,2,128]{4,3,2,1,0:T(2,128)(2,1)}) %all-reduce.15.cloned.1.call-update) | async-done | bytes 524304 | tf_op jit(solution)/shard_map/psum | solution.py:160
  363.9 4.6 collective-permute-start.10
  371.7 4.6 collective-permute-start.11
  390.8 5.1 collective-permute-start.13
  404.4 3.9 collective-permute-start.15
  412.1 46.1 %collective-permute-done.15 = bf16[4,1,18,64,128]{4,3,2,1,0:T(8,128)(2,1)} collective-permute-done((bf16[4,1,18,64,128]{4,3,2,1,0:T(8,128)(2,1)}, bf16[4,1,18,64,128]{4,3,2,1,0:T(8,128)(2,1)}, u32[]{:S(2)}, u32[]{:S(2)}) %collective-permute-start.15) | collective-permute-done | bytes 1179680 | tf_op jit(solution)/shard_map/ppermute | solution.py:12
  458.2 4.0 collective-permute-done.16
  465.9 9.6 %copy.238 = f32[4,4,18,128,27,2]{3,5,2,1,0,4:T(2,128)S(1)} copy(f32[4,4,18,128,27,2]{3,4,5,2,1,0:T(8,128)S(1)} %fusion.9) | data formatting | bytes 15925248 | tf_op jit(solution)/shard_map/prlie,tio->prltoe/dot_general | solution.py:129
  479.7 13.3 %all_gather.7 = bf16[4,2,128,2,128]{4,3,2,1,0:T(2,128)(2,1)} all-gather(bf16[4,2,16,2,128]{4,3,2,1,0:T(2,128)(2,1)S(1)} %get-tuple-element.6), channel_id=1, replica_groups=mesh['cascade'=2,'coil'=8,'readout'=8] {'coil'}, dimensions={2}, use_global_device_ids=true | all-gather | bytes 589824 | tf_op jit(solution)/shard_map/all_gather | solution.py:204
  497.7 8.8 %collective-permute-done.17 = bf16[4,2,128,2,128]{4,3,2,1,0:T(2,128)(2,1)} collective-permute-done((bf16[4,2,128,2,128]{4,3,2,1,0:T(2,128)(2,1)}, bf16[4,2,128,2,128]{4,3,2,1,0:T(2,128)(2,1)}, u32[]{:S(2)}, u32[]{:S(2)}) %collective-permute-start.17) | collective-permute-done | bytes 524320 | tf_op jit(solution)/shard_map/ppermute | solution.py:23
  524.0 59.3 %all-reduce.17.cloned.1.call-done = bf16[4,2,128,2,128]{4,3,2,1,0:T(2,128)(2,1)} async-done(((bf16[4,2,128,2,128]{4,3,2,1,0:T(2,128)(2,1)}), bf16[4,2,128,2,128]{4,3,2,1,0:T(2,128)(2,1)}) %all-reduce.17.cloned.1.call-update) | async-done | bytes 524304 | tf_op jit(solution)/shard_map/psum | solution.py:160
  584.2 4.0 collective-permute-start.18
  593.3 4.6 collective-permute-start.20
  612.3 3.9 collective-permute-start.22
  618.2 4.3 collective-permute-done.23
  624.3 3.9 collective-permute-start.24
  632.0 47.2 %collective-permute-done.24 = bf16[4,1,18,64,128]{4,3,2,1,0:T(8,128)(2,1)} collective-permute-done((bf16[4,1,18,64,128]{4,3,2,1,0:T(8,128)(2,1)}, bf16[4,1,18,64,128]{4,3,2,1,0:T(8,128)(2,1)}, u32[]{:S(2)}, u32[]{:S(2)}) %collective-permute-start.24) | collective-permute-done | bytes 1179680 | tf_op jit(solution)/shard_map/ppermute | solution.py:12
  685.7 9.6 %copy.237 = f32[4,4,18,128,27,2]{3,5,2,1,0,4:T(2,128)S(1)} copy(f32[4,4,18,128,27,2]{3,4,5,2,1,0:T(8,128)S(1)} %fusion.18) | data formatting | bytes 15925248 | tf_op jit(solution)/shard_map/prlie,tio->prltoe/dot_general | solution.py:129
  695.2 4.0 fusion.231
  (307 shorter events, 199.6 us)
Async XLA Ops:
  6.5 234.6 %copy-start = (bf16[1,27,64,2]{2,3,1,0:T(2,128)(2,1)S(1)}, bf16[1,27,64,2]{2,3,1,0:T(2,128)(2,1)}, u32[]{:S(2)}) copy-start(bf16[1,27,64,2]{2,3,1,0:T(2,128)(2,1)} %param.13) | copy-start | bytes 20740
  6.5 135.5 %all-reduce.13.cloned.1.call-start = ((), (), s32[]{:S(2)}) async-start(), calls=%async_computation | async-start | bytes 1048576 | tf_op jit(solution)/shard_map/psum | solution.py:160
  81.4 78.6 %copy-start.30 = (bf16[1,27,2,64]{3,2,1,0:T(2,128)(2,1)S(1)}, bf16[1,27,2,64]{3,2,1,0:T(2,128)(2,1)}, u32[]{:S(2)}) copy-start(bf16[1,27,2,64]{3,2,1,0:T(2,128)(2,1)} %param.11) | copy-start | bytes 20740
  82.9 280.1 %all-reduce.15.cloned.1.call-start = ((), (), s32[]{:S(2)}) async-start(), calls=%async_computation.1 | async-start | bytes 1048576 | tf_op jit(solution)/shard_map/psum | solution.py:160
  142.9 6.5 collective-permute-start
  146.9 4.9 collective-permute-start.1
  152.1 7.9 %collective-permute-start.2 = (bf16[4,1,18,2,128]{4,3,2,1,0:T(2,128)(2,1)S(1)}, bf16[4,1,18,2,128]{4,3,2,1,0:T(2,128)(2,1)S(1)}, u32[]{:S(2)}, u32[]{:S(2)}) collective-permute-start(bf16[4,1,18,2,128]{4,3,2,1,0:T(2,128)(2,1)S(1)} %get-tuple-element.61), channel_id=1, source_target_pairs={{0,1},{1,2},{2,3},{3,4},{4,5},{5,6},{6,7},{8,9},{9,10},{10,11},{11... | collective-permute-start | bytes 110600 | tf_op jit(solution)/shard_map/ppermute | solution.py:12
  156.7 6.2 collective-permute-start.3
  170.6 5.9 collective-permute-start.4
  174.5 6.3 collective-permute-start.5
  183.3 54.9 %collective-permute-start.6 = (bf16[4,1,18,64,128]{4,3,2,1,0:T(8,128)(2,1)}, bf16[4,1,18,64,128]{4,3,2,1,0:T(8,128)(2,1)}, u32[]{:S(2)}, u32[]{:S(2)}) collective-permute-start(bf16[4,1,18,64,128]{4,3,2,1,0:T(8,128)(2,1)} %get-tuple-element.19), channel_id=1, source_target_pairs={{0,1},{1,2},{2,3},{3,4},{4,5},{5,6},{6,7},{8,9},{9,10},{10,11},{11... | collective-permute-start | bytes 3538952 | tf_op jit(solution)/shard_map/ppermute | solution.py:12
  187.3 53.9 %collective-permute-start.7 = (bf16[4,1,18,64,128]{4,3,2,1,0:T(8,128)(2,1)S(1)}, bf16[4,1,18,64,128]{4,3,2,1,0:T(8,128)(2,1)}, u32[]{:S(2)}, u32[]{:S(2)}) collective-permute-start(bf16[4,1,18,64,128]{4,3,2,1,0:T(8,128)(2,1)S(1)} %get-tuple-element.20), channel_id=1, source_target_pairs={{1,0},{2,1},{3,2},{4,3},{5,4},{6,5},{7,6},{9,8},{10,9},{11,10},{12... | collective-permute-start | bytes 3538952 | tf_op jit(solution)/shard_map/ppermute | solution.py:15
  271.6 13.6 %collective-permute-start.8 = (bf16[4,2,128,2,128]{4,3,2,1,0:T(2,128)(2,1)}, bf16[4,2,128,2,128]{4,3,2,1,0:T(2,128)(2,1)}, u32[]{:S(2)}, u32[]{:S(2)}) collective-permute-start(bf16[4,2,128,2,128]{4,3,2,1,0:T(2,128)(2,1)} %all_gather.6), channel_id=1, source_target_pairs={{0,64},{1,65},{2,66},{3,67},{4,68},{5,69},{6,70},{7,71},{8,72},{9,... | collective-permute-start | bytes 1572872 | tf_op jit(solution)/shard_map/ppermute | solution.py:23
  302.9 280.4 %all-reduce.17.cloned.1.call-start = ((), (), s32[]{:S(2)}) async-start(), calls=%async_computation.2 | async-start | bytes 1048576 | tf_op jit(solution)/shard_map/psum | solution.py:160
  363.9 6.5 collective-permute-start.10
  368.4 3.1 collective-permute-start.9
  371.7 8.1 %collective-permute-start.11 = (bf16[4,1,18,2,128]{4,3,2,1,0:T(2,128)(2,1)S(1)}, bf16[4,1,18,2,128]{4,3,2,1,0:T(2,128)(2,1)S(1)}, u32[]{:S(2)}, u32[]{:S(2)}) collective-permute-start(bf16[4,1,18,2,128]{4,3,2,1,0:T(2,128)(2,1)S(1)} %get-tuple-element.57), channel_id=1, source_target_pairs={{0,1},{1,2},{2,3},{3,4},{4,5},{5,6},{6,7},{8,9},{9,10},{10,11},{11... | collective-permute-start | bytes 110600 | tf_op jit(solution)/shard_map/ppermute | solution.py:12
  376.3 6.3 collective-permute-start.12
  390.8 8.2 %collective-permute-start.13 = (bf16[4,2,1,64,128]{4,3,2,1,0:T(8,128)(2,1)S(1)}, bf16[4,2,1,64,128]{4,3,2,1,0:T(8,128)(2,1)S(1)}, u32[]{:S(2)}, u32[]{:S(2)}) collective-permute-start(bf16[4,2,1,64,128]{4,3,2,1,0:T(8,128)(2,1)S(1)} %get-tuple-element.26), channel_id=1, source_target_pairs={{0,8},{8,16},{16,24},{24,32},{32,40},{40,48},{48,56},{1,9},{9,17},... | collective-permute-start | bytes 393224 | tf_op jit(solution)/shard_map/ppermute | solution.py:12
  395.9 6.3 collective-permute-start.14
  404.4 53.8 %collective-permute-start.15 = (bf16[4,1,18,64,128]{4,3,2,1,0:T(8,128)(2,1)}, bf16[4,1,18,64,128]{4,3,2,1,0:T(8,128)(2,1)}, u32[]{:S(2)}, u32[]{:S(2)}) collective-permute-start(bf16[4,1,18,64,128]{4,3,2,1,0:T(8,128)(2,1)} %get-tuple-element.17), channel_id=1, source_target_pairs={{0,1},{1,2},{2,3},{3,4},{4,5},{5,6},{6,7},{8,9},{9,10},{10,11},{11... | collective-permute-start | bytes 3538952 | tf_op jit(solution)/shard_map/ppermute | solution.py:12
  408.3 53.8 %collective-permute-start.16 = (bf16[4,1,18,64,128]{4,3,2,1,0:T(8,128)(2,1)}, bf16[4,1,18,64,128]{4,3,2,1,0:T(8,128)(2,1)}, u32[]{:S(2)}, u32[]{:S(2)}) collective-permute-start(bf16[4,1,18,64,128]{4,3,2,1,0:T(8,128)(2,1)} %get-tuple-element.18), channel_id=1, source_target_pairs={{1,0},{2,1},{3,2},{4,3},{5,4},{6,5},{7,6},{9,8},{10,9},{11,10},{12... | collective-permute-start | bytes 3538952 | tf_op jit(solution)/shard_map/ppermute | solution.py:15
  475.5 20.6 %copy-start.4 = (bf16[1,2,4,2,128,2,128]{6,5,4,3,2,1,0:T(2,128)(2,1)S(1)}, bf16[1,2,4,2,128,2,128]{6,5,4,3,2,1,0:T(2,128)(2,1)}, u32[]{:S(2)}) copy-start(bf16[1,2,4,2,128,2,128]{6,5,4,3,2,1,0:T(2,128)(2,1)} %get-tuple-element.23) | copy-start | bytes 3145732
  493.0 13.6 %collective-permute-start.17 = (bf16[4,2,128,2,128]{4,3,2,1,0:T(2,128)(2,1)}, bf16[4,2,128,2,128]{4,3,2,1,0:T(2,128)(2,1)}, u32[]{:S(2)}, u32[]{:S(2)}) collective-permute-start(bf16[4,2,128,2,128]{4,3,2,1,0:T(2,128)(2,1)} %all_gather.7), channel_id=1, source_target_pairs={{0,64},{1,65},{2,66},{3,67},{4,68},{5,69},{6,70},{7,71},{8,72},{9,... | collective-permute-start | bytes 1572872 | tf_op jit(solution)/shard_map/ppermute | solution.py:23
  584.2 6.5 collective-permute-start.18
  588.2 4.9 collective-permute-start.19
  593.3 7.9 %collective-permute-start.20 = (bf16[4,1,18,2,128]{4,3,2,1,0:T(2,128)(2,1)S(1)}, bf16[4,1,18,2,128]{4,3,2,1,0:T(2,128)(2,1)S(1)}, u32[]{:S(2)}, u32[]{:S(2)}) collective-permute-start(bf16[4,1,18,2,128]{4,3,2,1,0:T(2,128)(2,1)S(1)} %get-tuple-element.53), channel_id=1, source_target_pairs={{0,1},{1,2},{2,3},{3,4},{4,5},{5,6},{6,7},{8,9},{9,10},{10,11},{11... | collective-permute-start | bytes 110600 | tf_op jit(solution)/shard_map/ppermute | solution.py:12
  598.0 6.2 collective-permute-start.21
  612.3 5.9 collective-permute-start.22
  616.2 6.3 collective-permute-start.23
  624.3 54.9 %collective-permute-start.24 = (bf16[4,1,18,64,128]{4,3,2,1,0:T(8,128)(2,1)}, bf16[4,1,18,64,128]{4,3,2,1,0:T(8,128)(2,1)}, u32[]{:S(2)}, u32[]{:S(2)}) collective-permute-start(bf16[4,1,18,64,128]{4,3,2,1,0:T(8,128)(2,1)} %get-tuple-element.15), channel_id=1, source_target_pairs={{0,1},{1,2},{2,3},{3,4},{4,5},{5,6},{6,7},{8,9},{9,10},{10,11},{11... | collective-permute-start | bytes 3538952 | tf_op jit(solution)/shard_map/ppermute | solution.py:12
  628.3 53.9 %collective-permute-start.25 = (bf16[4,1,18,64,128]{4,3,2,1,0:T(8,128)(2,1)S(1)}, bf16[4,1,18,64,128]{4,3,2,1,0:T(8,128)(2,1)}, u32[]{:S(2)}, u32[]{:S(2)}) collective-permute-start(bf16[4,1,18,64,128]{4,3,2,1,0:T(8,128)(2,1)S(1)} %get-tuple-element.16), channel_id=1, source_target_pairs={{1,0},{2,1},{3,2},{4,3},{5,4},{6,5},{7,6},{9,8},{10,9},{11,10},{12... | collective-permute-start | bytes 3538952 | tf_op jit(solution)/shard_map/ppermute | solution.py:15
  (28 other events, 147.6 us)
Sparse Core Ops, SparseCore 0:
  83.0 58.9 all-reduce.12
  303.0 59.8 all-reduce.14
  524.2 59.0 all-reduce.16
where the time goes:
time: 713 us; the launch traced here: 706 us
  waiting for transfers between devices  369 us (52%)
  local copies, waits for them, and re-layouts  132 us (19%)
  starting transfers between devices  92.6 us (13%)
  matrix products  37.7 us (5%)
  other arithmetic  32.4 us (5%)
  blocking collectives  26.6 us (4%)
  between operations  14.9 us (2%)
    psum x3, waiting for transfers between devices, cascade(): summed = lax.psum(terms.astype(jnp.bfloat16), 'coil').astype(jnp.float32)  178 us
    ppermute x12, waiting for transfers between devices, extended(): lax.ppermute(lax.slice_in_dim(block, block.shape[dim] - width, None, axis...  142 us
    ppermute x12, starting transfers between devices, extended(): lax.ppermute(lax.slice_in_dim(block, block.shape[dim] - width, None, axis...  48.5 us
    ppermute x12, starting transfers between devices, extended(): lax.ppermute(lax.slice_in_dim(block, 0, width, axis=dim), axis, backward)  37.7 us
    ppermute x12, waiting for transfers between devices, extended(): lax.ppermute(lax.slice_in_dim(block, 0, width, axis=dim), axis, backward)  35.2 us
    convert_element_type x2, local copies, waits for them, and re-layouts, row_matrix(): return blocks.reshape(2 * length, 2 * length).astype(jnp.bfloat16)  26.9 us
    all_gather x2, blocking collectives, per_device(): assembled = lax.all_gather(output, 'coil', axis=2, tiled=True)  26.6 us
    dot_general x2, local copies, waits for them, and re-layouts, project(): jnp.einsum('prlie,tio->prltoe', edged, weights, preferred_element_type=jn...  19.1 us
  transfers between devices with their start and end apart: 29, of which 20 were waited for; matrix products, arithmetic and copies ran while one was open for 1% of the time, Pallas kernels for 0%

commit v1 on v0

--- a/solution.py
+++ b/solution.py
@@ -2,6 +2,12 @@
 import jax.numpy as jnp
 from jax import lax
 from jax.sharding import PartitionSpec as P
+
+
+def summed_here(block, axis):
+    parts = lax.all_gather(block, axis, axis=0, tiled=False)
+    result = parts.sum(axis=0)
+    return result
 
 
 def extended(block, sides, width):
@@ -157,7 +163,7 @@
     back_half = along_rows(mixed, inverse_rows).astype(jnp.bfloat16)
     restored = along_columns(back_half, inverse_columns)
     terms = jnp.sum(multiply(coil_maps[:, None], restored, True), axis=0)
-    summed = lax.psum(terms.astype(jnp.bfloat16), "coil").astype(jnp.float32)
+    summed = summed_here(terms.astype(jnp.bfloat16), "coil").astype(jnp.float32)
     line_share = summed.shape[2] // lax.axis_size("coil")
     combined = lax.dynamic_slice_in_dim(summed, lax.axis_index("coil") * line_share, line_share, 2)
     combined = combined.astype(jnp.bfloat16)

time: 713 us -> 629 us (0.88)
  waiting for transfers between devices: 369 us -> 296 us
  local copies, waits for them, and re-layouts: 132 us -> 122 us
    psum x3 -> x0, waiting for transfers between devices: 178 us -> none  [cascade(): summed = lax.psum(terms.astype(jnp.bfloat16), 'coil').astype(jnp.float32)]
    all_gather x0 -> x3, waiting for transfers between devices: none -> 102 us  [summed_here(): parts = lax.all_gather(block, axis, axis=0, tiled=False)]
    transpose x1 -> x0, local copies, waits for them, and re-layouts: 9.56 us -> none  [project(): jnp.einsum('prlie,tio->prltoe', edged, weights, preferred_element_type=jn...]
    reduce_sum x0 -> x3, other arithmetic: none -> 8.86 us  [summed_here(): result = parts.sum(axis=0)]
    dot_general x2 -> x3, local copies, waits for them, and re-layouts: 19.1 us -> 25.4 us  [project(): jnp.einsum('prlie,tio->prltoe', edged, weights, preferred_element_type=jn...]
where the time goes in v1:
time: 629 us; the launch traced here: 621 us
  waiting for transfers between devices  296 us (47%)
  local copies, waits for them, and re-layouts  122 us (19%)
  starting transfers between devices  86.5 us (14%)
  matrix products  44.3 us (7%)
  other arithmetic  31.8 us (5%)
  blocking collectives  26.5 us (4%)
  between operations  14.8 us (2%)
    ppermute x12, waiting for transfers between devices, extended(): lax.ppermute(lax.slice_in_dim(block, block.shape[dim] - width, None, axis...  142 us
    all_gather x3, waiting for transfers between devices, summed_here(): parts = lax.all_gather(block, axis, axis=0, tiled=False)  102 us
    ppermute x12, starting transfers between devices, extended(): lax.ppermute(lax.slice_in_dim(block, block.shape[dim] - width, None, axis...  46.3 us
    ppermute x12, waiting for transfers between devices, extended(): lax.ppermute(lax.slice_in_dim(block, 0, width, axis=dim), axis, backward)  37.1 us
    ppermute x12, starting transfers between devices, extended(): lax.ppermute(lax.slice_in_dim(block, 0, width, axis=dim), axis, backward)  33.8 us
    convert_element_type x2, local copies, waits for them, and re-layouts, row_matrix(): return blocks.reshape(2 * length, 2 * length).astype(jnp.bfloat16)  26.9 us
    all_gather x2, blocking collectives, per_device(): assembled = lax.all_gather(output, 'coil', axis=2, tiled=True)  26.5 us
    dot_general x3, local copies, waits for them, and re-layouts, project(): jnp.einsum('prlie,tio->prltoe', edged, weights, preferred_element_type=jn...  25.4 us
  transfers between devices with their start and end apart: 29, of which 20 were waited for; matrix products, arithmetic and copies ran while one was open for 1% of the time, Pallas kernels for 0%

profile of v1, /device:TPU:35, one launch (start us, length us, event | category | flops | bytes accessed | tf_op | source)
XLA Modules:
  0.0 621.3 jit_solution(18316035264572097617)
XLA Ops:
  27.8 6.1 copy.228
  33.9 13.1 %reshape.491 = bf16[256,256,1]{1,0,2:T(8,128)(2,1)S(1)} reshape(bf16[128,2,128,2]{3,2,1,0:T(8,128)(2,1)} %copy.228) | data formatting | bytes 262144 | tf_op jit(solution)/shard_map/convert_element_type | solution.py:45
  47.0 6.1 copy.232
  53.1 13.8 %reshape.492 = bf16[256,256,1]{1,0,2:T(8,128)(2,1)} reshape(bf16[128,2,128,2]{3,2,1,0:T(8,128)(2,1)} %copy.232) | data formatting | bytes 262144 | tf_op jit(solution)/shard_map/convert_element_type | solution.py:45
  84.4 33.6 %all-gather.7.cloned.1.call-done = bf16[32,2,128,2,128]{4,2,3,1,0:T(8,128)(2,1)} async-done(((bf16[4,2,128,2,128]{4,2,3,1,0:T(8,128)(2,1)}), bf16[32,2,128,2,128]{4,2,3,1,0:T(8,128)(2,1)}) %all-gather.7.cloned.1.call-update) | async-done | bytes 4194320 | tf_op jit(solution)/shard_map/all_gather | solution.py:8
  129.1 4.6 collective-permute-start.2
  151.1 4.3 collective-permute-done.5
  157.9 3.9 collective-permute-start.6
  165.8 47.4 %collective-permute-done.6 = bf16[4,1,18,64,128]{4,3,2,1,0:T(8,128)(2,1)} collective-permute-done((bf16[4,1,18,64,128]{4,3,2,1,0:T(8,128)(2,1)}, bf16[4,1,18,64,128]{4,3,2,1,0:T(8,128)(2,1)}, u32[]{:S(2)}, u32[]{:S(2)}) %collective-permute-start.6) | collective-permute-done | bytes 1179680 | tf_op jit(solution)/shard_map/ppermute | solution.py:18
  215.6 6.0 fusion
  221.7 8.5 %copy.325 = f32[4,4,18,128,27,2]{3,2,5,1,0,4:T(8,128)S(1)} copy(f32[4,4,18,128,27,2]{3,4,5,2,1,0:T(8,128)} %fusion) | data formatting | bytes 15925248 | tf_op jit(solution)/shard_map/prlie,tio->prltoe/dot_general | solution.py:135
  231.8 13.2 %all_gather.19 = bf16[4,2,128,2,128]{4,2,3,1,0:T(8,128)(2,1)} all-gather(bf16[4,2,16,2,128]{4,2,3,1,0:T(8,128)(2,1)S(1)} %get-tuple-element.8), channel_id=1, replica_groups=mesh['cascade'=2,'coil'=8,'readout'=8] {'coil'}, dimensions={2}, use_global_device_ids=true | all-gather | bytes 589824 | tf_op jit(solution)/shard_map/all_gather | solution.py:210
  253.3 5.4 collective-permute-done.8
  274.7 34.4 %all-gather.9.cloned.1.call-done = bf16[32,2,128,2,128]{4,2,3,1,0:T(8,128)(2,1)} async-done(((bf16[4,2,128,2,128]{4,2,3,1,0:T(8,128)(2,1)}), bf16[32,2,128,2,128]{4,2,3,1,0:T(8,128)(2,1)}) %all-gather.9.cloned.1.call-update) | async-done | bytes 4194320 | tf_op jit(solution)/shard_map/all_gather | solution.py:8
  318.6 4.6 collective-permute-start.11
  335.6 5.6 collective-permute-start.13
  343.1 4.3 collective-permute-done.14
  349.7 3.9 collective-permute-start.15
  353.6 4.2 collective-permute-start.16
  357.8 46.8 %collective-permute-done.15 = bf16[4,1,18,64,128]{4,3,2,1,0:T(8,128)(2,1)} collective-permute-done((bf16[4,1,18,64,128]{4,3,2,1,0:T(8,128)(2,1)}, bf16[4,1,18,64,128]{4,3,2,1,0:T(8,128)(2,1)}, u32[]{:S(2)}, u32[]{:S(2)}) %collective-permute-start.15) | collective-permute-done | bytes 1179680 | tf_op jit(solution)/shard_map/ppermute | solution.py:18
  407.5 6.0 fusion.9
  413.5 8.5 %copy.324 = f32[4,4,18,128,27,2]{3,2,5,1,0,4:T(8,128)S(1)} copy(f32[4,4,18,128,27,2]{3,4,5,2,1,0:T(8,128)} %fusion.9) | data formatting | bytes 15925248 | tf_op jit(solution)/shard_map/prlie,tio->prltoe/dot_general | solution.py:135
  424.3 13.3 %all_gather.21 = bf16[4,2,128,2,128]{4,2,3,1,0:T(8,128)(2,1)} all-gather(bf16[4,2,16,2,128]{4,2,3,1,0:T(8,128)(2,1)S(1)} %get-tuple-element.6), channel_id=1, replica_groups=mesh['cascade'=2,'coil'=8,'readout'=8] {'coil'}, dimensions={2}, use_global_device_ids=true | all-gather | bytes 589824 | tf_op jit(solution)/shard_map/all_gather | solution.py:210
  442.4 8.8 %collective-permute-done.17 = bf16[4,2,128,2,128]{4,2,3,1,0:T(8,128)(2,1)} collective-permute-done((bf16[4,2,128,2,128]{4,2,3,1,0:T(8,128)(2,1)}, bf16[4,2,128,2,128]{4,2,3,1,0:T(8,128)(2,1)}, u32[]{:S(2)}, u32[]{:S(2)}) %collective-permute-start.17) | collective-permute-done | bytes 524320 | tf_op jit(solution)/shard_map/ppermute | solution.py:29
  466.9 33.7 %all-gather.11.cloned.1.call-done = bf16[32,2,128,2,128]{4,2,3,1,0:T(8,128)(2,1)} async-done(((bf16[4,2,128,2,128]{4,2,3,1,0:T(8,128)(2,1)}), bf16[32,2,128,2,128]{4,2,3,1,0:T(8,128)(2,1)}) %all-gather.11.cloned.1.call-update) | async-done | bytes 4194320 | tf_op jit(solution)/shard_map/all_gather | solution.py:8
  511.7 4.6 collective-permute-start.20
  519.5 3.9 collective-permute-done.21
  534.3 4.1 collective-permute-done.23
  540.2 3.9 collective-permute-start.24
  547.9 47.5 %collective-permute-done.24 = bf16[4,1,18,64,128]{4,3,2,1,0:T(8,128)(2,1)} collective-permute-done((bf16[4,1,18,64,128]{4,3,2,1,0:T(8,128)(2,1)}, bf16[4,1,18,64,128]{4,3,2,1,0:T(8,128)(2,1)}, u32[]{:S(2)}, u32[]{:S(2)}) %collective-permute-start.24) | collective-permute-done | bytes 1179680 | tf_op jit(solution)/shard_map/ppermute | solution.py:18
  598.0 5.7 fusion.18
  603.7 8.5 %copy.323 = f32[4,4,18,128,27,2]{3,2,5,1,0,4:T(8,128)S(1)} copy(f32[4,4,18,128,27,2]{3,4,5,2,1,0:T(8,128)} %fusion.18) | data formatting | bytes 15925248 | tf_op jit(solution)/shard_map/prlie,tio->prltoe/dot_general | solution.py:135
  (315 shorter events, 187.8 us)
Async XLA Ops:
  6.5 209.1 %copy-start = (bf16[1,27,64,2]{2,3,1,0:T(2,128)(2,1)S(1)}, bf16[1,27,64,2]{2,3,1,0:T(2,128)(2,1)}, u32[]{:S(2)}) copy-start(bf16[1,27,64,2]{2,3,1,0:T(2,128)(2,1)} %param.13) | copy-start | bytes 20740
  6.5 111.4 %all-gather.7.cloned.1.call-start = ((), (), s32[]{:S(2)}) async-start(), calls=%async_computation | async-start | bytes 4718592 | tf_op jit(solution)/shard_map/all_gather | solution.py:8
  84.3 224.8 %all-gather.9.cloned.1.call-start = ((), (), s32[]{:S(2)}) async-start(), calls=%async_computation.1 | async-start | bytes 4718592 | tf_op jit(solution)/shard_map/all_gather | solution.py:8
  120.9 21.1 %copy-start.23 = (bf16[4,2,128,2,128]{4,2,3,1,0:T(8,128)(2,1)}, bf16[4,2,128,2,128]{4,2,3,1,0:T(8,128)(2,1)S(1)}, u32[]{:S(2)}) copy-start(bf16[4,2,128,2,128]{4,2,3,1,0:T(8,128)(2,1)S(1)} %reduce_sum.64) | copy-start | bytes 1572868
  121.0 5.0 collective-permute-start
  124.1 5.0 collective-permute-start.1
  129.1 8.3 %collective-permute-start.2 = (bf16[4,1,18,2,128]{4,2,3,1,0:T(8,128)(2,1)S(1)}, bf16[4,1,18,2,128]{4,2,3,1,0:T(8,128)(2,1)S(1)}, u32[]{:S(2)}, u32[]{:S(2)}) collective-permute-start(bf16[4,1,18,2,128]{4,2,3,1,0:T(8,128)(2,1)S(1)} %get-tuple-element.58), channel_id=1, source_target_pairs={{0,1},{1,2},{2,3},{3,4},{4,5},{5,6},{6,7},{8,9},{9,10},{10,11},{11... | collective-permute-start | bytes 110600 | tf_op jit(solution)/shard_map/ppermute | solution.py:18
  133.7 7.0 %collective-permute-start.3 = (bf16[4,1,18,2,128]{4,2,3,1,0:T(8,128)(2,1)S(1)}, bf16[4,1,18,2,128]{4,2,3,1,0:T(8,128)(2,1)S(1)}, u32[]{:S(2)}, u32[]{:S(2)}) collective-permute-start(bf16[4,1,18,2,128]{4,2,3,1,0:T(8,128)(2,1)S(1)} %get-tuple-element.59), channel_id=1, source_target_pairs={{1,0},{2,1},{3,2},{4,3},{5,4},{6,5},{7,6},{9,8},{10,9},{11,10},{12... | collective-permute-start | bytes 110600 | tf_op jit(solution)/shard_map/ppermute | solution.py:21
  146.4 4.7 collective-permute-start.4
  149.1 6.3 %collective-permute-start.5 = (bf16[4,2,1,64,128]{4,3,2,1,0:T(8,128)(2,1)S(1)}, bf16[4,2,1,64,128]{4,3,2,1,0:T(8,128)(2,1)S(1)}, u32[]{:S(2)}, u32[]{:S(2)}) collective-permute-start(bf16[4,2,1,64,128]{4,3,2,1,0:T(8,128)(2,1)S(1)} %get-tuple-element.29), channel_id=1, source_target_pairs={{8,0},{16,8},{24,16},{32,24},{40,32},{48,40},{56,48},{9,1},{17,9},... | collective-permute-start | bytes 393224 | tf_op jit(solution)/shard_map/ppermute | solution.py:21
  157.9 55.2 %collective-permute-start.6 = (bf16[4,1,18,64,128]{4,3,2,1,0:T(8,128)(2,1)}, bf16[4,1,18,64,128]{4,3,2,1,0:T(8,128)(2,1)}, u32[]{:S(2)}, u32[]{:S(2)}) collective-permute-start(bf16[4,1,18,64,128]{4,3,2,1,0:T(8,128)(2,1)} %get-tuple-element.19), channel_id=1, source_target_pairs={{0,1},{1,2},{2,3},{3,4},{4,5},{5,6},{6,7},{8,9},{9,10},{10,11},{11... | collective-permute-start | bytes 3538952 | tf_op jit(solution)/shard_map/ppermute | solution.py:18
  161.8 53.8 %collective-permute-start.7 = (bf16[4,1,18,64,128]{4,3,2,1,0:T(8,128)(2,1)S(1)}, bf16[4,1,18,64,128]{4,3,2,1,0:T(8,128)(2,1)}, u32[]{:S(2)}, u32[]{:S(2)}) collective-permute-start(bf16[4,1,18,64,128]{4,3,2,1,0:T(8,128)(2,1)S(1)} %get-tuple-element.20), channel_id=1, source_target_pairs={{1,0},{2,1},{3,2},{4,3},{5,4},{6,5},{7,6},{9,8},{10,9},{11,10},{12... | collective-permute-start | bytes 3538952 | tf_op jit(solution)/shard_map/ppermute | solution.py:21
  245.1 13.6 %collective-permute-start.8 = (bf16[4,2,128,2,128]{4,2,3,1,0:T(8,128)(2,1)}, bf16[4,2,128,2,128]{4,2,3,1,0:T(8,128)(2,1)}, u32[]{:S(2)}, u32[]{:S(2)}) collective-permute-start(bf16[4,2,128,2,128]{4,2,3,1,0:T(8,128)(2,1)} %all_gather.19), channel_id=1, source_target_pairs={{0,64},{1,65},{2,66},{3,67},{4,68},{5,69},{6,70},{7,71},{8,72},{9,... | collective-permute-start | bytes 1572872 | tf_op jit(solution)/shard_map/ppermute | solution.py:29
  274.6 226.0 %all-gather.11.cloned.1.call-start = ((), (), s32[]{:S(2)}) async-start(), calls=%async_computation.2 | async-start | bytes 4718592 | tf_op jit(solution)/shard_map/all_gather | solution.py:8
  312.1 5.6 collective-permute-start.10
  314.3 4.2 collective-permute-start.9
  318.6 8.0 %collective-permute-start.11 = (bf16[4,1,18,2,128]{4,2,3,1,0:T(8,128)(2,1)S(1)}, bf16[4,1,18,2,128]{4,2,3,1,0:T(8,128)(2,1)S(1)}, u32[]{:S(2)}, u32[]{:S(2)}) collective-permute-start(bf16[4,1,18,2,128]{4,2,3,1,0:T(8,128)(2,1)S(1)} %get-tuple-element.56), channel_id=1, source_target_pairs={{0,1},{1,2},{2,3},{3,4},{4,5},{5,6},{6,7},{8,9},{9,10},{10,11},{11... | collective-permute-start | bytes 110600 | tf_op jit(solution)/shard_map/ppermute | solution.py:18
  323.2 6.3 %collective-permute-start.12 = (bf16[4,1,18,2,128]{4,2,3,1,0:T(8,128)(2,1)S(1)}, bf16[4,1,18,2,128]{4,2,3,1,0:T(8,128)(2,1)S(1)}, u32[]{:S(2)}, u32[]{:S(2)}) collective-permute-start(bf16[4,1,18,2,128]{4,2,3,1,0:T(8,128)(2,1)S(1)} %get-tuple-element.57), channel_id=1, source_target_pairs={{1,0},{2,1},{3,2},{4,3},{5,4},{6,5},{7,6},{9,8},{10,9},{11,10},{12... | collective-permute-start | bytes 110600 | tf_op jit(solution)/shard_map/ppermute | solution.py:21
  335.6 7.6 %collective-permute-start.13 = (bf16[4,2,1,64,128]{4,3,2,1,0:T(8,128)(2,1)S(1)}, bf16[4,2,1,64,128]{4,3,2,1,0:T(8,128)(2,1)S(1)}, u32[]{:S(2)}, u32[]{:S(2)}) collective-permute-start(bf16[4,2,1,64,128]{4,3,2,1,0:T(8,128)(2,1)S(1)} %get-tuple-element.26), channel_id=1, source_target_pairs={{0,8},{8,16},{16,24},{24,32},{32,40},{40,48},{48,56},{1,9},{9,17},... | collective-permute-start | bytes 393224 | tf_op jit(solution)/shard_map/ppermute | solution.py:18
  341.2 6.3 %collective-permute-start.14 = (bf16[4,2,1,64,128]{4,3,2,1,0:T(8,128)(2,1)S(1)}, bf16[4,2,1,64,128]{4,3,2,1,0:T(8,128)(2,1)S(1)}, u32[]{:S(2)}, u32[]{:S(2)}) collective-permute-start(bf16[4,2,1,64,128]{4,3,2,1,0:T(8,128)(2,1)S(1)} %get-tuple-element.27), channel_id=1, source_target_pairs={{8,0},{16,8},{24,16},{32,24},{40,32},{48,40},{56,48},{9,1},{17,9},... | collective-permute-start | bytes 393224 | tf_op jit(solution)/shard_map/ppermute | solution.py:21
  349.7 54.9 %collective-permute-start.15 = (bf16[4,1,18,64,128]{4,3,2,1,0:T(8,128)(2,1)}, bf16[4,1,18,64,128]{4,3,2,1,0:T(8,128)(2,1)}, u32[]{:S(2)}, u32[]{:S(2)}) collective-permute-start(bf16[4,1,18,64,128]{4,3,2,1,0:T(8,128)(2,1)} %get-tuple-element.17), channel_id=1, source_target_pairs={{0,1},{1,2},{2,3},{3,4},{4,5},{5,6},{6,7},{8,9},{9,10},{10,11},{11... | collective-permute-start | bytes 3538952 | tf_op jit(solution)/shard_map/ppermute | solution.py:18
  353.6 53.9 %collective-permute-start.16 = (bf16[4,1,18,64,128]{4,3,2,1,0:T(8,128)(2,1)}, bf16[4,1,18,64,128]{4,3,2,1,0:T(8,128)(2,1)}, u32[]{:S(2)}, u32[]{:S(2)}) collective-permute-start(bf16[4,1,18,64,128]{4,3,2,1,0:T(8,128)(2,1)} %get-tuple-element.18), channel_id=1, source_target_pairs={{1,0},{2,1},{3,2},{4,3},{5,4},{6,5},{7,6},{9,8},{10,9},{11,10},{12... | collective-permute-start | bytes 3538952 | tf_op jit(solution)/shard_map/ppermute | solution.py:21
  437.6 13.6 %collective-permute-start.17 = (bf16[4,2,128,2,128]{4,2,3,1,0:T(8,128)(2,1)}, bf16[4,2,128,2,128]{4,2,3,1,0:T(8,128)(2,1)}, u32[]{:S(2)}, u32[]{:S(2)}) collective-permute-start(bf16[4,2,128,2,128]{4,2,3,1,0:T(8,128)(2,1)} %all_gather.21), channel_id=1, source_target_pairs={{0,64},{1,65},{2,66},{3,67},{4,68},{5,69},{6,70},{7,71},{8,72},{9,... | collective-permute-start | bytes 1572872 | tf_op jit(solution)/shard_map/ppermute | solution.py:29
  503.6 21.1 %copy-start.22 = (bf16[4,2,128,2,128]{4,2,3,1,0:T(8,128)(2,1)}, bf16[4,2,128,2,128]{4,2,3,1,0:T(8,128)(2,1)S(1)}, u32[]{:S(2)}) copy-start(bf16[4,2,128,2,128]{4,2,3,1,0:T(8,128)(2,1)S(1)} %reduce_sum.68) | copy-start | bytes 1572868
  503.6 5.0 collective-permute-start.18
  506.7 5.0 collective-permute-start.19
  511.7 7.7 %collective-permute-start.20 = (bf16[4,1,18,2,128]{4,2,3,1,0:T(8,128)(2,1)S(1)}, bf16[4,1,18,2,128]{4,2,3,1,0:T(8,128)(2,1)S(1)}, u32[]{:S(2)}, u32[]{:S(2)}) collective-permute-start(bf16[4,1,18,2,128]{4,2,3,1,0:T(8,128)(2,1)S(1)} %get-tuple-element.54), channel_id=1, source_target_pairs={{0,1},{1,2},{2,3},{3,4},{4,5},{5,6},{6,7},{8,9},{9,10},{10,11},{11... | collective-permute-start | bytes 110600 | tf_op jit(solution)/shard_map/ppermute | solution.py:18
  516.4 7.0 %collective-permute-start.21 = (bf16[4,1,18,2,128]{4,2,3,1,0:T(8,128)(2,1)S(1)}, bf16[4,1,18,2,128]{4,2,3,1,0:T(8,128)(2,1)S(1)}, u32[]{:S(2)}, u32[]{:S(2)}) collective-permute-start(bf16[4,1,18,2,128]{4,2,3,1,0:T(8,128)(2,1)S(1)} %get-tuple-element.55), channel_id=1, source_target_pairs={{1,0},{2,1},{3,2},{4,3},{5,4},{6,5},{7,6},{9,8},{10,9},{11,10},{12... | collective-permute-start | bytes 110600 | tf_op jit(solution)/shard_map/ppermute | solution.py:21
  529.4 4.9 collective-permute-start.22
  532.1 6.3 %collective-permute-start.23 = (bf16[4,2,1,64,128]{4,3,2,1,0:T(8,128)(2,1)S(1)}, bf16[4,2,1,64,128]{4,3,2,1,0:T(8,128)(2,1)S(1)}, u32[]{:S(2)}, u32[]{:S(2)}) collective-permute-start(bf16[4,2,1,64,128]{4,3,2,1,0:T(8,128)(2,1)S(1)} %get-tuple-element.22), channel_id=1, source_target_pairs={{8,0},{16,8},{24,16},{32,24},{40,32},{48,40},{56,48},{9,1},{17,9},... | collective-permute-start | bytes 393224 | tf_op jit(solution)/shard_map/ppermute | solution.py:21
  540.2 55.2 %collective-permute-start.24 = (bf16[4,1,18,64,128]{4,3,2,1,0:T(8,128)(2,1)}, bf16[4,1,18,64,128]{4,3,2,1,0:T(8,128)(2,1)}, u32[]{:S(2)}, u32[]{:S(2)}) collective-permute-start(bf16[4,1,18,64,128]{4,3,2,1,0:T(8,128)(2,1)} %get-tuple-element.15), channel_id=1, source_target_pairs={{0,1},{1,2},{2,3},{3,4},{4,5},{5,6},{6,7},{8,9},{9,10},{10,11},{11... | collective-permute-start | bytes 3538952 | tf_op jit(solution)/shard_map/ppermute | solution.py:18
  544.2 53.8 %collective-permute-start.25 = (bf16[4,1,18,64,128]{4,3,2,1,0:T(8,128)(2,1)S(1)}, bf16[4,1,18,64,128]{4,3,2,1,0:T(8,128)(2,1)}, u32[]{:S(2)}, u32[]{:S(2)}) collective-permute-start(bf16[4,1,18,64,128]{4,3,2,1,0:T(8,128)(2,1)S(1)} %get-tuple-element.16), channel_id=1, source_target_pairs={{1,0},{2,1},{3,2},{4,3},{5,4},{6,5},{7,6},{9,8},{10,9},{11,10},{12... | collective-permute-start | bytes 3538952 | tf_op jit(solution)/shard_map/ppermute | solution.py:21
  (32 other events, 191.3 us)
Sparse Core Ops, SparseCore 0:
  84.4 33.4 all-gather.6
  274.8 34.3 all-gather.8
  467.1 33.5 all-gather.10
